TPU v7x, 128 devices: a whole 4x4x4 slice. The times are simulated.
128 devices in a mesh: psg: 32 (over y, z, core), qry: 4 (over x).
Axes of the slice: x: 4, y: 4, z: 4, core: 2. Of those that a mesh axis runs over, the one named last changes fastest.
Arguments:
- queries: bfloat16 [512, 32, 128], P(('psg', 'qry')), may hold values from -6 to 6
- passages: bfloat16 [1024, 256, 128], P('psg'), may hold values from -6 to 6
- candidates: int32 [512, 32], P(('psg', 'qry')), may hold values from 0 to 1023, as said below
- teacher: float32 [512, 32], P(('psg', 'qry')), may hold values from -8 to 8
Outputs:
- pair_loss: float32 [512], P(('psg', 'qry'))
- grad_queries: bfloat16 [512, 32, 128], P(('psg', 'qry'))
- grad_passages: bfloat16 [1024, 256, 128], P('psg', 'qry')
Inputs may be any that keep to these rules, and one draw needn't show every extreme that they name: Passage p lies in block p // 32. Among the 4 x 32 candidates of one device's queries (aligned blocks of 4 rows), at most 10 lie in one passage block; one passage block, the same for all devices, holds exactly 10 of every device's candidates. Candidate ids of one query may repeat.
All inputs are finite; a program needn't handle non-finite values.
Results may differ from a plain program's by a relative error of at most 0.019.
Values may be sent and summed in bfloat16 or wider, within the bound.
A program may use at most 64 MiB of HBM per device.

v0:
```python
import math
import jax
import jax.numpy as jnp
from jax import lax
from jax.sharding import PartitionSpec as P

epsilon = 1e-06
softness_scale = 0.05


def normalize(values):
    widened = values.astype(jnp.float32)
    inverse_norm = lax.rsqrt(jnp.sum(widened * widened, -1, keepdims=True) + epsilon)
    return (widened * inverse_norm, inverse_norm)


def select_rows(row_ids, table):
    row_total = table.shape[0]
    picker = (row_ids[:, None] == lax.iota(jnp.int32, row_total)[None, :]).astype(jnp.bfloat16)
    flat_table = table.reshape(row_total, -1)
    chosen = jnp.dot(picker, flat_table, preferred_element_type=jnp.float32).astype(jnp.bfloat16)
    return chosen.reshape((row_ids.shape[0],) + table.shape[1:])


def add_rows(accum, row_ids, delta):
    row_total = accum.shape[0]
    placer = (row_ids[:, None] == lax.iota(jnp.int32, row_total)[None, :]).astype(jnp.float32)
    flat_delta = delta.reshape(row_ids.shape[0], -1)
    added = jnp.einsum("sr,sx->rx", placer, flat_delta, precision=lax.Precision.HIGHEST)
    return accum + added.reshape(accum.shape)


def shards(queries, passages, candidates, teacher):
    query_count, query_tokens, feature_count = queries.shape
    pass_count, passage_tokens, _ = passages.shape
    cand_count = candidates.shape[1]
    owner_count = lax.axis_size("psg")
    capacity = max(2, (5 * query_count * cand_count + 2 * owner_count - 1) // (2 * owner_count))
    slot_count = owner_count * capacity
    pair_count = query_count * cand_count
    query_unit, query_inverse = normalize(queries)
    passage_unit, passage_inverse = normalize(passages)
    query_norm = query_unit.astype(jnp.bfloat16)
    passage_norm = passage_unit.astype(jnp.bfloat16)
    owner_ids = (candidates // pass_count).reshape(-1)
    local_ids = (candidates % pass_count).reshape(-1)
    onehot = (owner_ids[:, None] == lax.iota(jnp.int32, owner_count)[None, :]).astype(jnp.int32)
    before = jnp.cumsum(onehot, 0) - onehot
    rank_in_owner = jnp.sum(before * onehot, 1)
    slot_ids = owner_ids * capacity + rank_in_owner
    query_local = lax.iota(jnp.int32, pair_count) // cand_count
    slot_code = (
        jnp.zeros((slot_count,), jnp.int32)
        .at[slot_ids]
        .set(query_local * pass_count + local_ids + 1)
    )
    send_code = slot_code.reshape(owner_count, capacity)
    sender = lax.iota(jnp.int32, slot_count) // capacity
    received_label = lax.all_to_all(send_code, "psg", split_axis=0, concat_axis=0, tiled=True)
    query_rows = lax.all_gather(query_norm, "psg", axis=0, tiled=True)
    flat_peek = received_label.reshape(-1)
    fetch_rows = sender * query_count + jnp.where(flat_peek > 0, (flat_peek - 1) // pass_count, 0)
    flat_code = received_label.reshape(-1)
    live = flat_code > 0
    pass_index = jnp.where(live, (flat_code - 1) % pass_count, 0)
    target_rows = sender * query_count + jnp.where(live, (flat_code - 1) // pass_count, 0)
    block_len = math.gcd(slot_count, 64)
    block_total = slot_count // block_len

    def block_terms(offset):
        row_ids = lax.dynamic_slice_in_dim(fetch_rows, offset, block_len)
        passage_ids = lax.dynamic_slice_in_dim(pass_index, offset, block_len)
        query_tile = select_rows(row_ids, query_rows)
        passage_tile = select_rows(passage_ids, passage_norm)
        token_products = jnp.einsum(
            "sqe,spe->sqp", query_tile, passage_tile, preferred_element_type=jnp.float32
        )
        power_value = jnp.exp(token_products / softness_scale)
        return (query_tile, passage_tile, passage_ids, power_value, jnp.sum(power_value, -1))

    def forward_block(offset):
        reduced_sum = block_terms(offset)[4]
        return jnp.sum(softness_scale * jnp.log(reduced_sum), -1)

    offsets = lax.iota(jnp.int32, block_total) * block_len
    slot_scores = lax.map(forward_block, offsets).reshape(owner_count, capacity)
    scores_home = lax.all_to_all(slot_scores, "psg", split_axis=0, concat_axis=0, tiled=True)
    scores = scores_home.reshape(-1)[slot_ids].reshape(query_count, cand_count)
    teacher_exp = jnp.exp(teacher)
    mentor_score_sum = jnp.sum(teacher_exp, -1, keepdims=True)
    target = teacher_exp / mentor_score_sum
    log_target = teacher - jnp.log(mentor_score_sum)
    score_exp = jnp.exp(scores)
    score_total = jnp.sum(score_exp, -1, keepdims=True)
    likelihood = score_exp / score_total
    pair_loss = jnp.sum(target * (log_target - scores), -1) + jnp.log(score_total[:, 0])
    score_grad = likelihood - target
    send_grad = jnp.zeros((slot_count,), jnp.float32).at[slot_ids].set(score_grad.reshape(-1))
    recv_grad = lax.all_to_all(
        send_grad.reshape(owner_count, capacity), "psg", split_axis=0, concat_axis=0, tiled=True
    )
    flat_grad = recv_grad.reshape(-1)

    def backward(step_index, running):
        query_accum, passage_accum = running
        offset = step_index * block_len
        query_tile, passage_tile, passage_ids, power_value, reduced_sum = block_terms(offset)
        slot_grad = lax.dynamic_slice_in_dim(flat_grad, offset, block_len)
        weights = (slot_grad[:, None, None] * power_value / reduced_sum[:, :, None]).astype(
            jnp.bfloat16
        )
        query_delta = jnp.einsum(
            "sqp,spe->sqe", weights, passage_tile, preferred_element_type=jnp.float32
        )
        passage_delta = jnp.einsum(
            "sqp,sqe->spe", weights, query_tile, preferred_element_type=jnp.float32
        )
        home_rows = lax.dynamic_slice_in_dim(target_rows, offset, block_len)
        return (
            add_rows(query_accum, home_rows, query_delta),
            add_rows(passage_accum, passage_ids, passage_delta),
        )

    start_state = (
        jnp.zeros((owner_count * query_count, query_tokens, feature_count), jnp.float32),
        jnp.zeros((pass_count, passage_tokens, feature_count), jnp.float32),
    )
    query_accum, passage_accum = lax.fori_loop(0, block_total, backward, start_state)
    unit_query_grad = lax.psum_scatter(
        query_accum.astype(jnp.bfloat16), "psg", scatter_dimension=0, tiled=True
    ).astype(jnp.float32)
    unit_passage_grad = lax.psum_scatter(
        passage_accum.astype(jnp.bfloat16), "qry", scatter_dimension=1, tiled=True
    ).astype(jnp.float32)
    token_share = unit_passage_grad.shape[1]
    shard_start = lax.axis_index("qry") * token_share
    unit_slice = lax.dynamic_slice_in_dim(passage_unit, shard_start, token_share, 1)
    inverse_slice = lax.dynamic_slice_in_dim(passage_inverse, shard_start, token_share, 1)
    grad_queries = query_inverse * (
        unit_query_grad - query_unit * jnp.sum(query_unit * unit_query_grad, -1, keepdims=True)
    )
    grad_passages = inverse_slice * (
        unit_passage_grad - unit_slice * jnp.sum(unit_slice * unit_passage_grad, -1, keepdims=True)
    )
    return (pair_loss, grad_queries.astype(jnp.bfloat16), grad_passages.astype(jnp.bfloat16))


def solution(mesh):
    placed = (
        P(("psg", "qry"), None, None),
        P("psg", None, None),
        P(("psg", "qry"), None),
        P(("psg", "qry"), None),
    )
    return jax.shard_map(
        shards,
        mesh=mesh,
        in_specs=placed,
        out_specs=(P(("psg", "qry")), P(("psg", "qry"), None, None), P("psg", "qry", None)),
        check_vma=False,
    )
```

profile of v0, /device:TPU:1, one launch (start us, length us, event | category | flops | bytes accessed | tf_op | source)
XLA Modules:
  0.0 386.0 jit_solution(9751753425798929386)
XLA Ops:
  12.7 9.6 %all-to-all-start = ((s32[32,1,10]{2,1,0:T(1,128)}), s32[32,1,10]{2,1,0:T(1,128)S(1)}, u32[]{:S(2)}, u32[]{:S(2)}) async-start(s32[32,1,10]{2,1,0:T(1,128)} %bitcast.4), calls=%async_computation | async-start | bytes 32768 | tf_op jit(solution)/shard_map/all_to_all | solution.py:59
  22.3 2.9 fusion.34
  25.2 3.1 convert_multiply_fusion
  29.5 27.6 %all-gather.2.cloned.1.call-done = bf16[128,32,128]{2,1,0:T(8,128)(2,1)} async-done(((bf16[4,32,128]{2,1,0:T(8,128)(2,1)}), bf16[128,32,128]{2,1,0:T(8,128)(2,1)}) %all-gather.2.cloned.1.call-update) | async-done | bytes 1048592 | tf_op jit(solution)/shard_map/all_gather | solution.py:60
  57.1 44.8 %while.27 = (s32[]{:T(128)}, f32[5,64]{1,0:T(8,128)S(1)}, s32[5]{0:T(128)S(1)}, s32[320]{0:T(512)S(1)}, bf16[128,32,128]{2,1,0:T(8,128)(2,1)}, /*index=5*/s32[32...) while((s32[]{:T(128)}, f32[5,64]{1,0:T(8,128)S(1)}, s32[5]{0:T(128)S(1)}, ...), condition=%wide.region_9.10_spmd, body=%wide.region_6.9_spmd.sunk | while | flops 338964416 | bytes 22055336 | solution.py:86
  102.6 5.3 %all-to-all-start.1 = ((f32[32,1,10]{2,1,0:T(1,128)}), f32[32,1,10]{2,1,0:T(1,128)S(1)}, u32[]{:S(2)}, u32[]{:S(2)}) async-start(f32[32,1,10]{2,1,0:T(1,128)} %bitcast.5), calls=%async_computation.1 | async-start | bytes 32768 | tf_op jit(solution)/shard_map/all_to_all | solution.py:87
  108.1 6.8 %all-to-all-done.1 = f32[32,1,10]{2,1,0:T(1,128)S(1)} async-done(((f32[32,1,10]{2,1,0:T(1,128)}), f32[32,1,10]{2,1,0:T(1,128)S(1)}, u32[]{:S(2)}, u32[]{:S(2)}) %all-to-all-start.1) | async-done | bytes 1312 | tf_op jit(solution)/shard_map/all_to_all | solution.py:87
  119.6 4.1 %all-to-all-start.2 = ((f32[32,1,10]{2,1,0:T(1,128)}), f32[32,1,10]{2,1,0:T(1,128)S(1)}, u32[]{:S(2)}, u32[]{:S(2)}) async-start(f32[32,1,10]{2,1,0:T(1,128)} %bitcast.6), calls=%async_computation.2 | async-start | bytes 32768 | tf_op jit(solution)/shard_map/all_to_all | solution.py:99
  123.8 6.9 %all-to-all-done.2 = f32[32,1,10]{2,1,0:T(1,128)S(1)} async-done(((f32[32,1,10]{2,1,0:T(1,128)}), f32[32,1,10]{2,1,0:T(1,128)S(1)}, u32[]{:S(2)}, u32[]{:S(2)}) %all-to-all-start.2) | async-done | bytes 1312 | tf_op jit(solution)/shard_map/all_to_all | solution.py:99
  131.5 131.0 %while.28 = (s32[]{:T(128)}, f32[128,32,128]{2,0,1:T(8,128)}, f32[32,256,128]{2,0,1:T(8,128)}, s32[320]{0:T(512)S(1)}, f32[320]{0:T(512)S(1)}, /*index=5*/bf16[1...) while((s32[]{:T(128)}, f32[128,32,128]{2,0,1:T(8,128)}, ...), condition=%wide.region_15.16_spmd.clone, body=%wide.region_13.15_spmd.clone.sunk | while | flops 1822705664 | bytes 114847024 | solution.py:128
  139.6 2.6 select_add_fusion.4
  142.3 1.8 fusion.116
  145.3 10.6 %select_add_fusion.5 = f32[32,256,128]{2,0,1:T(8,128)S(1)} fusion(f32[32,256,128]{2,0,1:T(8,128)S(1)} %copy-done, pred[]{:T(512)S(6)} %compare.11, s32[64]{0:T(128)S(1)} %dynamic_slice.59, f32[8,8,256,128]{3,2,1,0:T(8,128)S(1)} %bitcast.149), kind=kOutput, calls=%fused_computation.23.clone.1 | convolution fusion | flops 807405568 | bytes 16777472 | tf_op jit(solution)/shard_map/while/body/eval_jaxpr/sr,sx->rx/dot_general | solution.py:29
  155.9 2.0 copy-done.1
  165.8 2.7 select_add_fusion.4
  171.4 10.6 %select_add_fusion.5 = f32[32,256,128]{2,0,1:T(8,128)S(1)} fusion(f32[32,256,128]{2,0,1:T(8,128)S(1)} %copy-done, pred[]{:T(512)S(6)} %compare.11, s32[64]{0:T(128)S(1)} %dynamic_slice.59, f32[8,8,256,128]{3,2,1,0:T(8,128)S(1)} %bitcast.149), kind=kOutput, calls=%fused_computation.23.clone.1 | convolution fusion | flops 807405568 | bytes 16777472 | tf_op jit(solution)/shard_map/while/body/eval_jaxpr/sr,sx->rx/dot_general | solution.py:29
  182.1 2.0 copy-done.1
  192.0 2.7 select_add_fusion.4
  197.6 10.6 %select_add_fusion.5 = f32[32,256,128]{2,0,1:T(8,128)S(1)} fusion(f32[32,256,128]{2,0,1:T(8,128)S(1)} %copy-done, pred[]{:T(512)S(6)} %compare.11, s32[64]{0:T(128)S(1)} %dynamic_slice.59, f32[8,8,256,128]{3,2,1,0:T(8,128)S(1)} %bitcast.149), kind=kOutput, calls=%fused_computation.23.clone.1 | convolution fusion | flops 807405568 | bytes 16777472 | tf_op jit(solution)/shard_map/while/body/eval_jaxpr/sr,sx->rx/dot_general | solution.py:29
  208.2 2.0 copy-done.1
  218.1 2.7 select_add_fusion.4
  223.7 10.6 %select_add_fusion.5 = f32[32,256,128]{2,0,1:T(8,128)S(1)} fusion(f32[32,256,128]{2,0,1:T(8,128)S(1)} %copy-done, pred[]{:T(512)S(6)} %compare.11, s32[64]{0:T(128)S(1)} %dynamic_slice.59, f32[8,8,256,128]{3,2,1,0:T(8,128)S(1)} %bitcast.149), kind=kOutput, calls=%fused_computation.23.clone.1 | convolution fusion | flops 807405568 | bytes 16777472 | tf_op jit(solution)/shard_map/while/body/eval_jaxpr/sr,sx->rx/dot_general | solution.py:29
  234.4 2.0 copy-done.1
  244.3 2.7 select_add_fusion.4
  249.9 10.6 %select_add_fusion.5 = f32[32,256,128]{2,0,1:T(8,128)S(1)} fusion(f32[32,256,128]{2,0,1:T(8,128)S(1)} %copy-done, pred[]{:T(512)S(6)} %compare.11, s32[64]{0:T(128)S(1)} %dynamic_slice.59, f32[8,8,256,128]{3,2,1,0:T(8,128)S(1)} %bitcast.149), kind=kOutput, calls=%fused_computation.23.clone.1 | convolution fusion | flops 807405568 | bytes 16777472 | tf_op jit(solution)/shard_map/while/body/eval_jaxpr/sr,sx->rx/dot_general | solution.py:29
  260.5 2.0 copy-done.1
  262.5 3.8 copy.86
  266.3 6.0 %copy.85 = bf16[32,256,128]{2,1,0:T(8,128)(2,1)} copy(f32[32,256,128]{2,0,1:T(8,128)} %get-tuple-element.206) | data formatting | bytes 6291456 | tf_op jit(solution)/shard_map/while | solution.py:128
  273.0 67.0 %reduce-scatter.3.cloned.1.call-done = bf16[4,32,128]{2,1,0:T(8,128)(2,1)} async-done(((bf16[128,32,128]{2,1,0:T(8,128)(2,1)}), bf16[4,32,128]{2,1,0:T(8,128)(2,1)}) %reduce-scatter.3.cloned.1.call-update) | async-done | bytes 32784 | tf_op jit(solution)/shard_map/reduce_scatter | solution.py:129
  340.0 2.0 fusion.43
  342.0 31.2 %reduce-scatter.5.cloned.1.call-done = bf16[32,64,128]{2,1,0:T(8,128)(2,1)} async-done(((bf16[32,256,128]{2,1,0:T(8,128)(2,1)}), bf16[32,64,128]{2,1,0:T(8,128)(2,1)}) %reduce-scatter.5.cloned.1.call-update) | async-done | bytes 524304 | tf_op jit(solution)/shard_map/reduce_scatter | solution.py:132
  373.2 6.3 %fusion.39 = bf16[32,64,128]{2,1,0:T(8,128)(2,1)} fusion(bf16[32,64,128]{2,1,0:T(8,128)(2,1)} %reduce-scatter.5.cloned.1.call-done, f32[32,256,128]{2,1,0:T(8,128)} %get-tuple-element.270, s32[]{:T(128)S(6)} %select_n.80, f32[32,64]{1,0:T(8,128)S(1)} %constant_dynamic-slice_fusion), kind=kOutput, calls=%fused_computation.59 | output fusion | flops 1837183 | bytes 3679232 | tf_op jit(solution)/shard_map/mul | solution.py:143
  (194 shorter events, 100.9 us)
Async XLA Ops:
  7.2 50.0 %all-gather.2.cloned.1.call-start = ((), (), s32[]{:S(2)}) async-start(), calls=%async_computation.5 | async-start | bytes 1081344 | tf_op jit(solution)/shard_map/all_gather | solution.py:60
  12.7 16.5 %all-to-all-start = ((s32[32,1,10]{2,1,0:T(1,128)}), s32[32,1,10]{2,1,0:T(1,128)S(1)}, u32[]{:S(2)}, u32[]{:S(2)}) async-start(s32[32,1,10]{2,1,0:T(1,128)} %bitcast.4), calls=%async_computation | async-start | bytes 32768 | tf_op jit(solution)/shard_map/all_to_all | solution.py:59
  22.3 3.0 copy-start.4
  57.1 50.8 %copy-start.6 = (f32[4,32]{1,0:T(4,128)S(1)}, f32[4,32]{1,0:T(4,128)}, u32[]{:S(2)}) copy-start(f32[4,32]{1,0:T(4,128)} %param.11) | copy-start | bytes 1540
  102.6 12.2 %all-to-all-start.1 = ((f32[32,1,10]{2,1,0:T(1,128)}), f32[32,1,10]{2,1,0:T(1,128)S(1)}, u32[]{:S(2)}, u32[]{:S(2)}) async-start(f32[32,1,10]{2,1,0:T(1,128)} %bitcast.5), calls=%async_computation.1 | async-start | bytes 32768 | tf_op jit(solution)/shard_map/all_to_all | solution.py:87
  119.6 11.2 %all-to-all-start.2 = ((f32[32,1,10]{2,1,0:T(1,128)}), f32[32,1,10]{2,1,0:T(1,128)S(1)}, u32[]{:S(2)}, u32[]{:S(2)}) async-start(f32[32,1,10]{2,1,0:T(1,128)} %bitcast.6), calls=%async_computation.2 | async-start | bytes 32768 | tf_op jit(solution)/shard_map/all_to_all | solution.py:99
  123.7 216.3 %reduce-scatter.3.cloned.1.call-start = ((), (), s32[]{:S(2)}) async-start(), calls=%async_computation.6 | async-start | bytes 1081344 | tf_op jit(solution)/shard_map/reduce_scatter | solution.py:129
  138.0 1.6 copy-start.2
  142.3 1.9 copy-start.3
  142.3 2.9 copy-start
  155.9 2.0 copy-start.1
  164.2 1.6 copy-start.2
  168.5 1.9 copy-start.3
  168.5 2.9 copy-start
  182.0 2.0 copy-start.1
  190.4 1.6 copy-start.2
  194.6 1.9 copy-start.3
  194.6 2.9 copy-start
  208.2 2.0 copy-start.1
  216.5 1.6 copy-start.2
  220.8 1.9 copy-start.3
  220.8 2.9 copy-start
  234.4 2.0 copy-start.1
  242.7 1.6 copy-start.2
  246.9 1.9 copy-start.3
  246.9 2.9 copy-start
  260.5 2.0 copy-start.1
  266.3 106.9 %reduce-scatter.5.cloned.1.call-start = ((), (), s32[]{:S(2)}) async-start(), calls=%async_computation.7 | async-start | bytes 2621440 | tf_op jit(solution)/shard_map/reduce_scatter | solution.py:132
  272.4 67.7 %copy-start.5 = (bf16[4,32,128]{2,1,0:T(8,128)(2,1)S(1)}, bf16[4,32,128]{2,1,0:T(8,128)(2,1)}, u32[]{:S(2)}) copy-start(bf16[4,32,128]{2,1,0:T(8,128)(2,1)} %param.8) | copy-start | bytes 98308
Sparse Core Ops, SparseCore 0:
  10.8 46.2 all-gather.1
  266.4 73.5 reduce-scatter.2
  342.4 30.7 reduce-scatter.4
where the time goes:
time: 388 us; the launch traced here: 386 us
  waiting for transfers between devices  140 us (36%)
  matrix products  129 us (33%)
  local copies, waits for them, and re-layouts  53 us (14%)
  other arithmetic  20.3 us (5%)
  starting transfers between devices  19.1 us (5%)
  between operations  14 us (4%)
  loops' own time  10.6 us (3%)
    reduce_scatter x1, waiting for transfers between devices, shards(): lax.psum_scatter(query_accum.astype(jnp.bfloat16), 'psg', scatter_dimensi...  67 us
    dot_general x10, matrix products, add_rows(): jnp.einsum('sr,sx->rx', placer, flat_delta, precision=lax.Precision.HIGHEST)  66.4 us
    dot_general x20, matrix products, select_rows(): jnp.dot(picker, flat_table, preferred_element_type=jnp.float32)  32.2 us
    reduce_scatter x1, waiting for transfers between devices, shards(): lax.psum_scatter(passage_accum.astype(jnp.bfloat16), 'qry', scatter_dimen...  31.2 us
    while x60, local copies, waits for them, and re-layouts  31.1 us
    all_gather x1, waiting for transfers between devices, shards(): query_rows = lax.all_gather(query_norm, 'psg', axis=0, tiled=True)  27.6 us
    dot_general x10, matrix products, block_terms(): jnp.einsum('sqe,spe->sqp', query_tile, passage_tile, preferred_element_ty...  16.2 us
    another operation x1, loops' own time, shards(): slot_scores = lax.map(forward_block, offsets).reshape(owner_count, capacity)  9.92 us
  transfers between devices with their start and end apart: 6, of which 6 were waited for; matrix products, arithmetic and copies ran while one was open for 5% of the time, Pallas kernels for 0%

commit v1 on v0

--- a/solution.py
+++ b/solution.py
@@ -57,7 +57,9 @@
     send_code = slot_code.reshape(owner_count, capacity)
     sender = lax.iota(jnp.int32, slot_count) // capacity
     received_label = lax.all_to_all(send_code, "psg", split_axis=0, concat_axis=0, tiled=True)
-    query_rows = lax.all_gather(query_norm, "psg", axis=0, tiled=True)
+    query_rows = jnp.concatenate(
+        lax.all_to_all(jnp.stack([query_norm] * lax.axis_size("psg")), "psg", 0, 0), axis=0
+    )
     flat_peek = received_label.reshape(-1)
     fetch_rows = sender * query_count + jnp.where(flat_peek > 0, (flat_peek - 1) // pass_count, 0)
     flat_code = received_label.reshape(-1)

time: 388 us -> 367 us (0.946)
  matrix products: 129 us -> 116 us
  waiting for transfers between devices: 140 us -> 127 us
    all_gather x1 -> x0, waiting for transfers between devices: 27.6 us -> none  [shards(): query_rows = lax.all_gather(query_norm, 'psg', axis=0, tiled=True)]
    all_to_all x0 -> x1, waiting for transfers between devices: none -> 12.8 us  [shards(): lax.all_to_all(jnp.stack([query_norm] * lax.axis_size('psg')), 'psg', 0, 0)]
    dot_general x20, matrix products: 32.2 us -> 20 us  [select_rows(): jnp.dot(picker, flat_table, preferred_element_type=jnp.float32)]
    all_to_all x0 -> x1, starting transfers between devices: none -> 4.98 us  [shards(): lax.all_to_all(jnp.stack([query_norm] * lax.axis_size('psg')), 'psg', 0, 0)]
where the time goes in v1:
time: 367 us; the launch traced here: 366 us
  waiting for transfers between devices  127 us (35%)
  matrix products  116 us (32%)
  local copies, waits for them, and re-layouts  54.2 us (15%)
  starting transfers between devices  22.7 us (6%)
  other arithmetic  20.2 us (6%)
  between operations  14.3 us (4%)
  loops' own time  10.6 us (3%)
    reduce_scatter x1, waiting for transfers between devices, shards(): lax.psum_scatter(query_accum.astype(jnp.bfloat16), 'psg', scatter_dimensi...  67.1 us
    dot_general x10, matrix products, add_rows(): jnp.einsum('sr,sx->rx', placer, flat_delta, precision=lax.Precision.HIGHEST)  66.4 us
    reduce_scatter x1, waiting for transfers between devices, shards(): lax.psum_scatter(passage_accum.astype(jnp.bfloat16), 'qry', scatter_dimen...  31.2 us
    while x60, local copies, waits for them, and re-layouts  31 us
    dot_general x20, matrix products, select_rows(): jnp.dot(picker, flat_table, preferred_element_type=jnp.float32)  20 us
    dot_general x10, matrix products, block_terms(): jnp.einsum('sqe,spe->sqp', query_tile, passage_tile, preferred_element_ty...  16.2 us
    all_to_all x1, waiting for transfers between devices, shards(): lax.all_to_all(jnp.stack([query_norm] * lax.axis_size('psg')), 'psg', 0, 0)  12.8 us
    another operation x1, loops' own time, shards(): slot_scores = lax.map(forward_block, offsets).reshape(owner_count, capacity)  9.92 us
  transfers between devices with their start and end apart: 6, of which 6 were waited for; matrix products, arithmetic and copies ran while one was open for 5% of the time, Pallas kernels for 0%

profile of v1, /device:TPU:1, one launch (start us, length us, event | category | flops | bytes accessed | tf_op | source)
XLA Modules:
  0.0 365.6 jit_solution(2701382802776870042)
XLA Ops:
  10.3 9.6 %all-to-all-start = ((s32[32,1,10]{2,1,0:T(1,128)}), s32[32,1,10]{2,1,0:T(1,128)S(1)}, u32[]{:S(2)}, u32[]{:S(2)}) async-start(s32[32,1,10]{2,1,0:T(1,128)} %bitcast.4), calls=%async_computation | async-start | bytes 32768 | tf_op jit(solution)/shard_map/all_to_all | solution.py:59
  21.6 2.7 fusion.34
  24.4 2.4 all-to-all-done
  28.0 5.0 %all-to-all-start.1 = ((bf16[32,4,32,128]{3,2,1,0:T(8,128)(2,1)}), bf16[32,4,32,128]{3,2,1,0:T(8,128)(2,1)S(1)}, u32[]{:S(2)}, u32[]{:S(2)}) async-start(bf16[32,4,32,128]{3,2,1,0:T(8,128)(2,1)} %stack.2), calls=%async_computation.1 | async-start | bytes 2097152 | tf_op jit(solution)/shard_map/all_to_all | solution.py:61
  33.0 3.8 %convert_multiply_fusion = (f32[32,256,128]{2,1,0:T(8,128)}, bf16[32,256,128]{2,1,0:T(8,128)(2,1)S(1)}) fusion(bf16[32,256,128]{2,1,0:T(8,128)(2,1)} %param.9, f32[32,256]{1,0:T(8,128)S(1)} %add_rsqrt_fusion), kind=kLoop, calls=%fused_computation.49 | loop fusion | flops 3145728 | bytes 8421376 | tf_op jit(solution)/shard_map/mul | solution.py:14
  37.1 12.8 %all-to-all-done.1 = bf16[32,4,32,128]{3,2,1,0:T(8,128)(2,1)S(1)} async-done(((bf16[32,4,32,128]{3,2,1,0:T(8,128)(2,1)}), bf16[32,4,32,128]{3,2,1,0:T(8,128)(2,1)S(1)}, u32[]{:S(2)}, u32[]{:S(2)}) %all-to-all-start.1) | async-done | bytes 1048608 | tf_op jit(solution)/shard_map/all_to_all | solution.py:61
  49.9 38.7 %while.27 = (s32[]{:T(128)}, f32[5,64]{1,0:T(8,128)S(1)}, s32[5]{0:T(128)S(1)}, s32[320]{0:T(512)S(1)}, bf16[32,4,32,128]{3,2,1,0:T(8,128)(2,1)S(1)}, /*index=5*...) while((s32[]{:T(128)}, f32[5,64]{1,0:T(8,128)S(1)}, ...), condition=%wide.region_9.10_spmd, body=%wide.region_6.9_spmd.sunk | while | flops 338964416 | bytes 22055336 | solution.py:88
  89.3 3.9 %all-to-all-start.2 = ((f32[32,1,10]{2,1,0:T(1,128)}), f32[32,1,10]{2,1,0:T(1,128)S(1)}, u32[]{:S(2)}, u32[]{:S(2)}) async-start(f32[32,1,10]{2,1,0:T(1,128)} %bitcast.5), calls=%async_computation.2 | async-start | bytes 32768 | tf_op jit(solution)/shard_map/all_to_all | solution.py:89
  93.4 6.8 %all-to-all-done.2 = f32[32,1,10]{2,1,0:T(1,128)S(1)} async-done(((f32[32,1,10]{2,1,0:T(1,128)}), f32[32,1,10]{2,1,0:T(1,128)S(1)}, u32[]{:S(2)}, u32[]{:S(2)}) %all-to-all-start.2) | async-done | bytes 1312 | tf_op jit(solution)/shard_map/all_to_all | solution.py:89
  104.8 4.1 %all-to-all-start.3 = ((f32[32,1,10]{2,1,0:T(1,128)}), f32[32,1,10]{2,1,0:T(1,128)S(1)}, u32[]{:S(2)}, u32[]{:S(2)}) async-start(f32[32,1,10]{2,1,0:T(1,128)} %bitcast.6), calls=%async_computation.3 | async-start | bytes 32768 | tf_op jit(solution)/shard_map/all_to_all | solution.py:101
  109.1 6.9 %all-to-all-done.3 = f32[32,1,10]{2,1,0:T(1,128)S(1)} async-done(((f32[32,1,10]{2,1,0:T(1,128)}), f32[32,1,10]{2,1,0:T(1,128)S(1)}, u32[]{:S(2)}, u32[]{:S(2)}) %all-to-all-start.3) | async-done | bytes 1312 | tf_op jit(solution)/shard_map/all_to_all | solution.py:101
  116.8 124.9 %while.28 = (s32[]{:T(128)}, f32[128,32,128]{2,0,1:T(8,128)}, f32[32,256,128]{2,0,1:T(8,128)}, s32[320]{0:T(512)S(1)}, f32[320]{0:T(512)S(1)}, /*index=5*/bf16[3...) while((s32[]{:T(128)}, f32[128,32,128]{2,0,1:T(8,128)}, ...), condition=%wide.region_15.16_spmd.clone, body=%wide.region_13.15_spmd.clone.sunk | while | flops 1822705664 | bytes 114847024 | solution.py:130
  123.7 2.6 select_add_fusion.4
  129.3 10.6 %select_add_fusion.5 = f32[32,256,128]{2,0,1:T(8,128)S(1)} fusion(f32[32,256,128]{2,0,1:T(8,128)S(1)} %copy-done, pred[]{:T(512)S(6)} %compare.11, s32[64]{0:T(128)S(1)} %dynamic_slice.59, f32[8,8,256,128]{3,2,1,0:T(8,128)S(1)} %bitcast.151), kind=kOutput, calls=%fused_computation.23.clone.1 | convolution fusion | flops 807405568 | bytes 16777472 | tf_op jit(solution)/shard_map/while/body/eval_jaxpr/sr,sx->rx/dot_general | solution.py:29
  140.0 2.0 copy-done.1
  148.7 2.6 select_add_fusion.4
  154.3 10.6 %select_add_fusion.5 = f32[32,256,128]{2,0,1:T(8,128)S(1)} fusion(f32[32,256,128]{2,0,1:T(8,128)S(1)} %copy-done, pred[]{:T(512)S(6)} %compare.11, s32[64]{0:T(128)S(1)} %dynamic_slice.59, f32[8,8,256,128]{3,2,1,0:T(8,128)S(1)} %bitcast.151), kind=kOutput, calls=%fused_computation.23.clone.1 | convolution fusion | flops 807405568 | bytes 16777472 | tf_op jit(solution)/shard_map/while/body/eval_jaxpr/sr,sx->rx/dot_general | solution.py:29
  164.9 2.0 copy-done.1
  173.6 2.6 select_add_fusion.4
  179.2 10.6 %select_add_fusion.5 = f32[32,256,128]{2,0,1:T(8,128)S(1)} fusion(f32[32,256,128]{2,0,1:T(8,128)S(1)} %copy-done, pred[]{:T(512)S(6)} %compare.11, s32[64]{0:T(128)S(1)} %dynamic_slice.59, f32[8,8,256,128]{3,2,1,0:T(8,128)S(1)} %bitcast.151), kind=kOutput, calls=%fused_computation.23.clone.1 | convolution fusion | flops 807405568 | bytes 16777472 | tf_op jit(solution)/shard_map/while/body/eval_jaxpr/sr,sx->rx/dot_general | solution.py:29
  189.8 2.0 copy-done.1
  198.5 2.6 select_add_fusion.4
  204.1 10.6 %select_add_fusion.5 = f32[32,256,128]{2,0,1:T(8,128)S(1)} fusion(f32[32,256,128]{2,0,1:T(8,128)S(1)} %copy-done, pred[]{:T(512)S(6)} %compare.11, s32[64]{0:T(128)S(1)} %dynamic_slice.59, f32[8,8,256,128]{3,2,1,0:T(8,128)S(1)} %bitcast.151), kind=kOutput, calls=%fused_computation.23.clone.1 | convolution fusion | flops 807405568 | bytes 16777472 | tf_op jit(solution)/shard_map/while/body/eval_jaxpr/sr,sx->rx/dot_general | solution.py:29
  214.8 2.0 copy-done.1
  223.5 2.6 select_add_fusion.4
  229.1 10.6 %select_add_fusion.5 = f32[32,256,128]{2,0,1:T(8,128)S(1)} fusion(f32[32,256,128]{2,0,1:T(8,128)S(1)} %copy-done, pred[]{:T(512)S(6)} %compare.11, s32[64]{0:T(128)S(1)} %dynamic_slice.59, f32[8,8,256,128]{3,2,1,0:T(8,128)S(1)} %bitcast.151), kind=kOutput, calls=%fused_computation.23.clone.1 | convolution fusion | flops 807405568 | bytes 16777472 | tf_op jit(solution)/shard_map/while/body/eval_jaxpr/sr,sx->rx/dot_general | solution.py:29
  241.7 3.8 %copy.86 = bf16[128,32,128]{2,1,0:T(8,128)(2,1)} copy(f32[128,32,128]{2,0,1:T(8,128)} %get-tuple-element.205) | data formatting | bytes 3145728 | tf_op jit(solution)/shard_map/while | solution.py:130
  245.5 6.0 %copy.85 = bf16[32,256,128]{2,1,0:T(8,128)(2,1)} copy(f32[32,256,128]{2,0,1:T(8,128)} %get-tuple-element.206) | data formatting | bytes 6291456 | tf_op jit(solution)/shard_map/while | solution.py:130
  252.2 67.1 %reduce-scatter.3.cloned.1.call-done = bf16[4,32,128]{2,1,0:T(8,128)(2,1)} async-done(((bf16[128,32,128]{2,1,0:T(8,128)(2,1)}), bf16[4,32,128]{2,1,0:T(8,128)(2,1)}) %reduce-scatter.3.cloned.1.call-update) | async-done | bytes 32784 | tf_op jit(solution)/shard_map/reduce_scatter | solution.py:131
  319.3 2.0 fusion.43
  321.2 31.2 %reduce-scatter.5.cloned.1.call-done = bf16[32,64,128]{2,1,0:T(8,128)(2,1)} async-done(((bf16[32,256,128]{2,1,0:T(8,128)(2,1)}), bf16[32,64,128]{2,1,0:T(8,128)(2,1)}) %reduce-scatter.5.cloned.1.call-update) | async-done | bytes 524304 | tf_op jit(solution)/shard_map/reduce_scatter | solution.py:134
  352.4 6.3 %fusion.39 = bf16[32,64,128]{2,1,0:T(8,128)(2,1)} fusion(bf16[32,64,128]{2,1,0:T(8,128)(2,1)} %reduce-scatter.5.cloned.1.call-done, f32[32,256,128]{2,1,0:T(8,128)} %get-tuple-element.270, s32[]{:T(128)S(6)} %select_n.80, f32[32,64]{1,0:T(8,128)S(1)} %constant_dynamic-slice_fusion), kind=kOutput, calls=%fused_computation.59 | output fusion | flops 1837183 | bytes 3679232 | tf_op jit(solution)/shard_map/mul | solution.py:145
  (192 shorter events, 92.2 us)
Async XLA Ops:
  10.3 16.5 %all-to-all-start = ((s32[32,1,10]{2,1,0:T(1,128)}), s32[32,1,10]{2,1,0:T(1,128)S(1)}, u32[]{:S(2)}, u32[]{:S(2)}) async-start(s32[32,1,10]{2,1,0:T(1,128)} %bitcast.4), calls=%async_computation | async-start | bytes 32768 | tf_op jit(solution)/shard_map/all_to_all | solution.py:59
  28.0 21.9 %all-to-all-start.1 = ((bf16[32,4,32,128]{3,2,1,0:T(8,128)(2,1)}), bf16[32,4,32,128]{3,2,1,0:T(8,128)(2,1)S(1)}, u32[]{:S(2)}, u32[]{:S(2)}) async-start(bf16[32,4,32,128]{3,2,1,0:T(8,128)(2,1)} %stack.2), calls=%async_computation.1 | async-start | bytes 2097152 | tf_op jit(solution)/shard_map/all_to_all | solution.py:61
  49.9 43.3 %copy-start.5 = (f32[4,32]{1,0:T(4,128)S(1)}, f32[4,32]{1,0:T(4,128)}, u32[]{:S(2)}) copy-start(f32[4,32]{1,0:T(4,128)} %param.11) | copy-start | bytes 1540
  89.3 10.8 %all-to-all-start.2 = ((f32[32,1,10]{2,1,0:T(1,128)}), f32[32,1,10]{2,1,0:T(1,128)S(1)}, u32[]{:S(2)}, u32[]{:S(2)}) async-start(f32[32,1,10]{2,1,0:T(1,128)} %bitcast.5), calls=%async_computation.2 | async-start | bytes 32768 | tf_op jit(solution)/shard_map/all_to_all | solution.py:89
  104.8 11.2 %all-to-all-start.3 = ((f32[32,1,10]{2,1,0:T(1,128)}), f32[32,1,10]{2,1,0:T(1,128)S(1)}, u32[]{:S(2)}, u32[]{:S(2)}) async-start(f32[32,1,10]{2,1,0:T(1,128)} %bitcast.6), calls=%async_computation.3 | async-start | bytes 32768 | tf_op jit(solution)/shard_map/all_to_all | solution.py:101
  109.0 210.3 %reduce-scatter.3.cloned.1.call-start = ((), (), s32[]{:S(2)}) async-start(), calls=%async_computation.6 | async-start | bytes 1081344 | tf_op jit(solution)/shard_map/reduce_scatter | solution.py:131
  122.1 1.6 copy-start.2
  126.4 1.9 copy-start.3
  126.4 2.9 copy-start
  140.0 2.0 copy-start.1
  147.0 1.6 copy-start.2
  151.3 1.9 copy-start.3
  151.3 2.9 copy-start
  164.9 2.0 copy-start.1
  172.0 1.6 copy-start.2
  176.2 1.9 copy-start.3
  176.3 2.9 copy-start
  189.8 2.0 copy-start.1
  196.9 1.6 copy-start.2
  201.2 1.9 copy-start.3
  201.2 2.9 copy-start
  214.8 2.0 copy-start.1
  221.9 1.6 copy-start.2
  226.1 1.9 copy-start.3
  226.1 2.9 copy-start
  239.7 2.0 copy-start.1
  245.5 106.9 %reduce-scatter.5.cloned.1.call-start = ((), (), s32[]{:S(2)}) async-start(), calls=%async_computation.7 | async-start | bytes 2621440 | tf_op jit(solution)/shard_map/reduce_scatter | solution.py:134
  251.5 67.7 %copy-start.4 = (bf16[4,32,128]{2,1,0:T(8,128)(2,1)S(1)}, bf16[4,32,128]{2,1,0:T(8,128)(2,1)}, u32[]{:S(2)}) copy-start(bf16[4,32,128]{2,1,0:T(8,128)(2,1)} %param.8) | copy-start | bytes 98308
Sparse Core Ops, SparseCore 0:
  245.6 73.6 reduce-scatter.2
  321.7 30.7 reduce-scatter.4
